TPU v7x, 32 devices: a whole 2x2x4 slice. The times are simulated.
32 devices in a mesh: group: 2 (over y), tm: 8 (over z, core), pix: 2 (over x), sub: 1.
Axes of the slice: x: 2, y: 2, z: 4, core: 2. Of those that a mesh axis runs over, the one named last changes fastest.
Arguments:
- anomaly: bfloat16 [512, 65536], P('tm', ('group', 'pix', 'sub')), parts along dimension 1, may hold values from -6 to 6
- offsets: int32 [32], replicated, may hold values from 0 to 256, as said below
- taper_index: int32 [32], replicated, may hold values from 0 to 3
Outputs:
- spectral_gram: float32 [256, 64, 64], P(('group', 'tm')), parts along dimension 0
- leading_energy: float32 [256], P(('group', 'tm')), parts along dimension 0
There are 2 independent parts, one for each index of `group`. A program takes and returns all parts, laid end to end along the dimension named above; an argument that names none is the same for every part. Nothing has to cross between parts.
Inputs may be any that keep to these rules, and one draw needn't show every extreme that they name: `offsets`: block starts never fall; the first block starts at day 0 and the last at day 512 - 256.
All inputs are finite; a program needn't handle non-finite values.
Results may differ from a plain program's by a relative error of at most 0.0034.
Values may be sent and summed in bfloat16 or wider, within the bound.
A program may use at most 128 MiB of HBM per device.

v0:
```python
import math
import jax
import jax.numpy as jnp
from jax import lax
from jax.sharding import PartitionSpec as P

NFFT = 256
NB = 32
POWER = 8
NF = 128
power_eps = 1e-06


def window_at(taper_index, steps_t, length):
    steps = steps_t.astype(jnp.float32)
    phase = steps * (2.0 * math.pi / length)
    center = (steps + 0.5) * (math.pi / length)
    hann = jnp.sin(center) ** 2
    hamming = 0.54 - 0.46 * jnp.cos(phase)
    blackman = 0.42 - 0.5 * jnp.cos(phase) + 0.08 * jnp.cos(2.0 * phase)
    sine_win = jnp.sin(center)
    which = taper_index[:, None]
    return jnp.where(
        which == 0, hann, jnp.where(which == 1, hamming, jnp.where(which == 2, blackman, sine_win))
    )


def day_operator(offsets, taper_index, freqs, days, length):
    day = jnp.arange(days, dtype=jnp.int32)
    step = day[None, :] - offsets[:, None]
    inside = (step >= 0) & (step < length)
    windows = jnp.where(inside, window_at(taper_index, step, length), 0.0)
    energy = 1.0 / jnp.sqrt(jnp.sum(windows * windows, axis=1, keepdims=True))
    scaled = windows * energy
    product = freqs[:, None, None] * step[None] & length - 1
    angle = product.astype(jnp.float32) * (2.0 * math.pi / length)
    table = jnp.stack([jnp.cos(angle), -jnp.sin(angle)], axis=1)
    table = lax.reduce_precision(table, 8, 7)
    return (table * scaled).reshape(freqs.shape[0], 2 * offsets.shape[0], days)


def shards(anomaly, offsets, taper_index):
    series = lax.all_to_all(anomaly, "tm", split_axis=1, concat_axis=0, tiled=True)
    days = series.shape[0]
    own = NF // lax.axis_size("tm")
    freqs = lax.axis_index("tm") * own + jnp.arange(own, dtype=jnp.int32)
    operator = day_operator(offsets, taper_index, freqs, days, NFFT)
    covariance = jnp.einsum("dp,ep->de", series, series, preferred_element_type=jnp.float32)
    covariance = lax.psum(covariance, ("tm", "pix", "sub"))
    total_pixels = anomaly.shape[1] * lax.axis_size(("pix", "sub"))
    half = jnp.einsum("fid,de->fie", operator, covariance, precision=lax.Precision.HIGH)
    spectral_gram = jnp.einsum("fie,fje->fij", half, operator, precision=lax.Precision.HIGH)
    spectral_gram = spectral_gram / total_pixels
    vector = jnp.ones((own, 2 * NB), jnp.float32)
    for _ in range(POWER):
        applied = jnp.einsum("fij,fj->fi", spectral_gram, vector, precision=lax.Precision.HIGHEST)
        vector = applied / jnp.sqrt(jnp.mean(applied * applied, axis=1, keepdims=True) + power_eps)
    applied = jnp.einsum("fij,fj->fi", spectral_gram, vector, precision=lax.Precision.HIGHEST)
    leading_energy = jnp.sqrt(jnp.mean(applied * applied, axis=1))
    return (spectral_gram, leading_energy)


def solution(mesh):
    placed = (P("tm", ("group", "pix", "sub")), P(), P())
    return jax.shard_map(
        shards,
        mesh=mesh,
        in_specs=placed,
        out_specs=(P(("group", "tm"), None, None), P(("group", "tm"))),
        check_vma=False,
    )
```

profile of v0, /device:TPU:0, one launch (start us, length us, event | category | flops | bytes accessed | tf_op | source)
XLA Modules:
  0.0 184.7 jit_solution(9127771249241529888)
XLA Ops:
  7.2 3.1 %copy.28 = bf16[8,8,8,2048]{3,2,0,1:T(8,128)(2,1)} copy(bf16[8,8,8,2048]{3,2,1,0:T(8,128)(2,1)} %bitcast.79) | data formatting | bytes 4194304 | tf_op jit(solution)/shard_map/all_to_all | solution.py:43
  10.3 6.5 %all-to-all-start = ((bf16[64,8,2048]{2,0,1:T(8,128)(2,1)}), bf16[64,8,2048]{2,0,1:T(8,128)(2,1)}, u32[]{:S(2)}, u32[]{:S(2)}) async-start(bf16[64,8,2048]{2,0,1:T(8,128)(2,1)} %bitcast.78), calls=%async_computation | async-start | bytes 4194304 | tf_op jit(solution)/shard_map/all_to_all | solution.py:43
  16.8 0.9 multiply_reduce_fusion
  17.8 3.8 %fusion.2 = (f32[16,1,32,512]{3,2,1,0:T(8,128)S(1)}, f32[16,1,32,512]{3,2,1,0:T(8,128)S(1)}) fusion(s32[32,512]{1,0:T(8,128)S(1)} %iota_subtract_fusion, s32[16]{0:T(128)S(1)} %iota_add_fusion), kind=kLoop, calls=%fused_computation.8 | loop fusion | flops 1310720 | bytes 2162752 | tf_op jit(solution)/shard_map/cos | solution.py:37
  21.6 44.3 %all-to-all-done = bf16[64,8,2048]{2,0,1:T(8,128)(2,1)} async-done(((bf16[64,8,2048]{2,0,1:T(8,128)(2,1)}), bf16[64,8,2048]{2,0,1:T(8,128)(2,1)}, u32[]{:S(2)}, u32[]{:S(2)}) %all-to-all-start) | async-done | bytes 2097184 | tf_op jit(solution)/shard_map/all_to_all | solution.py:43
  65.9 4.5 %fusion.6 = f32[512,512]{1,0:T(8,128)} fusion(bf16[512,2048]{1,0:T(8,128)(2,1)} %bitcast.3), kind=kOutput, calls=%fused_computation.46 | convolution fusion | flops 1073741824 | bytes 3145728 | tf_op jit(solution)/shard_map/dp,ep->de/dot_general | solution.py:48
  70.4 0.8 broadcast_multiply_fusion
  71.2 0.2 maximum_reduce-precision_fusion
  71.5 0.3 bitcast_multiply_fusion
  71.8 90.9 %all-reduce.2.cloned.1.call-done = f32[512,512]{1,0:T(8,128)} async-done(((f32[512,512]{1,0:T(8,128)}), f32[512,512]{1,0:T(8,128)}) %all-reduce.2.cloned.1.call-update) | async-done | bytes 1048592 | tf_op jit(solution)/shard_map/psum | solution.py:49
  162.7 3.0 %fusion = f32[16,64,512]{2,1,0:T(8,128)S(1)} fusion(f32[16,64,512]{2,1,0:T(8,128)S(1)} %bitcast_multiply_fusion, f32[512,512]{1,0:T(8,128)} %all-reduce.2.cloned.1.call-done), kind=kOutput, calls=%fused_computation.4 | convolution fusion | flops 1610612736 | bytes 5242880 | tf_op jit(solution)/shard_map/fid,de->fie/dot_general | solution.py:51
  165.7 1.1 convolution_multiply_fusion
  166.9 0.9 fusion.7
  167.8 0.1 multiply_reduce_fusion.9
  168.0 0.9 fusion.8
  168.9 0.1 multiply_reduce_fusion.8
  169.2 0.9 fusion.9
  170.1 0.1 multiply_reduce_fusion.7
  170.3 1.1 fusion.10
  171.4 0.1 multiply_reduce_fusion.6
  171.6 0.9 fusion.11
  172.6 0.1 multiply_reduce_fusion.5
  172.8 0.9 fusion.12
  173.7 0.1 multiply_reduce_fusion.4
  173.9 0.9 fusion.13
  174.9 0.1 multiply_reduce_fusion.3
  175.1 0.9 fusion.14
  176.0 0.1 multiply_reduce_fusion.2
  176.2 0.1 broadcast_divide_fusion
  176.2 0.9 fusion.15
  177.2 0.1 multiply_reduce_fusion.1
  177.3 0.5 multiply_sqrt_fusion
  (29 shorter events, 0.8 us)
Async XLA Ops:
  10.3 6.5 %copy-start.2 = (s32[32]{0:T(128)S(1)}, s32[32]{0:T(128)}, u32[]{:S(2)}) copy-start(s32[32]{0:T(128)} %param.5) | copy-start | bytes 388
  10.3 6.5 %copy-start.1 = (s32[32]{0:T(128)S(1)}, s32[32]{0:T(128)}, u32[]{:S(2)}) copy-start(s32[32]{0:T(128)} %param.4) | copy-start | bytes 388
  10.3 55.6 %all-to-all-start = ((bf16[64,8,2048]{2,0,1:T(8,128)(2,1)}), bf16[64,8,2048]{2,0,1:T(8,128)(2,1)}, u32[]{:S(2)}, u32[]{:S(2)}) async-start(bf16[64,8,2048]{2,0,1:T(8,128)(2,1)} %bitcast.78), calls=%async_computation | async-start | bytes 4194304 | tf_op jit(solution)/shard_map/all_to_all | solution.py:43
  16.8 145.9 %all-reduce.2.cloned.1.call-start = ((), (), s32[]{:S(2)}) async-start(), calls=%async_computation.1 | async-start | bytes 2097152 | tf_op jit(solution)/shard_map/psum | solution.py:49
  166.8 9.4 %copy-start = (f32[16,64,64]{2,1,0:T(8,128)}, f32[16,64,64]{2,1,0:T(8,128)S(1)}, u32[]{:S(2)}) copy-start(f32[16,64,64]{2,1,0:T(8,128)S(1)} %convolution_multiply_fusion) | copy-start | bytes 786436
Sparse Core Ops, SparseCore 0:
  70.6 92.0 all-reduce.1
where the time goes:
time: 185 us
  waiting for transfers between devices  135 us (73%)
  matrix products  17.3 us (9%)
  between operations  14.2 us (8%)
  other arithmetic  8.3 us (4%)
  starting transfers between devices  6.49 us (4%)
  local copies, waits for them, and re-layouts  3.17 us (2%)
    psum x1, waiting for transfers between devices, shards(): covariance = lax.psum(covariance, ('tm', 'pix', 'sub'))  90.9 us
    all_to_all x1, waiting for transfers between devices, shards(): lax.all_to_all(anomaly, 'tm', split_axis=1, concat_axis=0, tiled=True)  44.3 us
    dot_general x9, matrix products, shards(): jnp.einsum('fij,fj->fi', spectral_gram, vector, precision=lax.Precision.H...  8.59 us
    all_to_all x1, starting transfers between devices, shards(): lax.all_to_all(anomaly, 'tm', split_axis=1, concat_axis=0, tiled=True)  6.46 us
    dot_general x1, matrix products, shards(): jnp.einsum('dp,ep->de', series, series, preferred_element_type=jnp.float32)  4.49 us
    cos x1, other arithmetic, day_operator(): table = jnp.stack([jnp.cos(angle), -jnp.sin(angle)], axis=1)  3.82 us
  transfers between devices with their start and end apart: 2, of which 2 were waited for; matrix products, arithmetic and copies ran while one was open for 3% of the time, Pallas kernels for 0%

commit v1 on v0

--- a/solution.py
+++ b/solution.py
@@ -46,7 +46,13 @@
     freqs = lax.axis_index("tm") * own + jnp.arange(own, dtype=jnp.int32)
     operator = day_operator(offsets, taper_index, freqs, days, NFFT)
     covariance = jnp.einsum("dp,ep->de", series, series, preferred_element_type=jnp.float32)
-    covariance = lax.psum(covariance, ("tm", "pix", "sub"))
+
+    def obtain_tokens(patch, dev_axis, peer_axis):
+        for b in (dev_axis, peer_axis):
+            patch = lax.psum(patch, axis_name=b)
+        return patch
+
+    covariance = obtain_tokens(covariance, ("pix", "sub"), "tm")
     total_pixels = anomaly.shape[1] * lax.axis_size(("pix", "sub"))
     half = jnp.einsum("fid,de->fie", operator, covariance, precision=lax.Precision.HIGH)
     spectral_gram = jnp.einsum("fie,fje->fij", half, operator, precision=lax.Precision.HIGH)

time: 185 us -> 189 us (1.022)
  blocking collectives: 0 us -> 55.2 us
  waiting for transfers between devices: 135 us -> 94.2 us
  starting transfers between devices: 6.49 us -> 0.08 us
  matrix products: 17.3 us -> 14.9 us
    all_to_all x0 -> x1, blocking collectives: none -> 55.2 us  [shards(): lax.all_to_all(anomaly, 'tm', split_axis=1, concat_axis=0, tiled=True)]
    all_to_all x1 -> x0, waiting for transfers between devices: 44.3 us -> none  [shards(): lax.all_to_all(anomaly, 'tm', split_axis=1, concat_axis=0, tiled=True)]
    all_to_all x1 -> x0, starting transfers between devices: 6.46 us -> none  [shards(): lax.all_to_all(anomaly, 'tm', split_axis=1, concat_axis=0, tiled=True)]
    psum x1 -> x2, waiting for transfers between devices: 90.9 us -> 94.2 us  [obtain_tokens(): patch = lax.psum(patch, axis_name=b)]
    dot_general x1, matrix products: 4.49 us -> 2.32 us  [shards(): jnp.einsum('dp,ep->de', series, series, preferred_element_type=jnp.float32)]
where the time goes in v1:
time: 189 us
  waiting for transfers between devices  94.2 us (50%)
  blocking collectives  55.2 us (29%)
  matrix products  14.9 us (8%)
  between operations  14.3 us (8%)
  other arithmetic  8.3 us (4%)
    psum x2, waiting for transfers between devices, obtain_tokens(): patch = lax.psum(patch, axis_name=b)  94.2 us
    all_to_all x1, blocking collectives, shards(): lax.all_to_all(anomaly, 'tm', split_axis=1, concat_axis=0, tiled=True)  55.2 us
    dot_general x9, matrix products, shards(): jnp.einsum('fij,fj->fi', spectral_gram, vector, precision=lax.Precision.H...  8.43 us
    cos x1, other arithmetic, day_operator(): table = jnp.stack([jnp.cos(angle), -jnp.sin(angle)], axis=1)  3.82 us
  transfers between devices with their start and end apart: 2, of which 2 were waited for; matrix products, arithmetic and copies ran while one was open for 3% of the time, Pallas kernels for 0%

profile of v1, /device:TPU:0, one launch (start us, length us, event | category | flops | bytes accessed | tf_op | source)
XLA Modules:
  0.0 188.7 jit_solution(14603781749783120951)
XLA Ops:
  7.2 1.7 copy.28
  8.9 55.2 %all_to_all.19 = bf16[64,8,2048]{2,0,1:T(8,128)(2,1)S(1)} all-to-all(bf16[64,8,2048]{2,0,1:T(8,128)(2,1)S(1)} %bitcast.79), channel_id=1, replica_groups=mesh['group'=2,'tm'=8,'pix'=2,'sub'=1] {'tm'}, dimensions={1} | all-to-all | bytes 4194304 | tf_op jit(solution)/shard_map/all_to_all | solution.py:43
  64.1 2.3 %fusion.6 = f32[512,512]{1,0:T(8,128)} fusion(bf16[512,2048]{1,0:T(8,128)(2,1)S(1)} %bitcast.81), kind=kOutput, calls=%fused_computation.46 | convolution fusion | flops 1073741824 | bytes 3145728 | tf_op jit(solution)/shard_map/dp,ep->de/dot_general | solution.py:48
  66.6 0.9 multiply_reduce_fusion
  67.5 3.8 %fusion.2 = (f32[16,1,32,512]{3,2,1,0:T(8,128)S(1)}, f32[16,1,32,512]{3,2,1,0:T(8,128)S(1)}) fusion(s32[32,512]{1,0:T(8,128)S(1)} %iota_subtract_fusion, s32[16]{0:T(128)S(1)} %iota_add_fusion), kind=kLoop, calls=%fused_computation.8 | loop fusion | flops 1310720 | bytes 2162752 | tf_op jit(solution)/shard_map/cos | solution.py:37
  71.4 34.2 %all-reduce.3.cloned.1.call-done = f32[512,512]{1,0:T(8,128)} async-done(((f32[512,512]{1,0:T(8,128)}), f32[512,512]{1,0:T(8,128)}) %all-reduce.3.cloned.1.call-update) | async-done | bytes 1048592 | tf_op jit(solution)/shard_map/psum | solution.py:52
  105.6 0.8 broadcast_multiply_fusion
  106.4 0.2 maximum_reduce-precision_fusion
  106.6 0.3 bitcast_multiply_fusion
  106.9 60.0 %all-reduce.5.cloned.1.call-done = f32[512,512]{1,0:T(8,128)} async-done(((f32[512,512]{1,0:T(8,128)}), f32[512,512]{1,0:T(8,128)}) %all-reduce.5.cloned.1.call-update) | async-done | bytes 1048592 | tf_op jit(solution)/shard_map/psum | solution.py:52
  166.9 3.1 %fusion = f32[16,64,512]{2,1,0:T(8,128)S(1)} fusion(f32[16,64,512]{2,1,0:T(8,128)S(1)} %bitcast_multiply_fusion, f32[512,512]{1,0:T(8,128)} %all-reduce.5.cloned.1.call-done), kind=kOutput, calls=%fused_computation.4 | convolution fusion | flops 1610612736 | bytes 5242880 | tf_op jit(solution)/shard_map/fid,de->fie/dot_general | solution.py:57
  170.0 1.1 convolution_multiply_fusion
  171.1 0.9 fusion.7
  172.0 0.1 multiply_reduce_fusion.9
  172.2 0.9 fusion.8
  173.2 0.1 multiply_reduce_fusion.8
  173.4 0.9 fusion.9
  174.3 0.1 multiply_reduce_fusion.7
  174.5 0.9 fusion.10
  175.5 0.1 multiply_reduce_fusion.6
  175.6 0.1 broadcast_divide_fusion.4
  175.7 0.9 fusion.11
  176.6 0.1 multiply_reduce_fusion.5
  176.8 0.9 fusion.12
  177.8 0.1 multiply_reduce_fusion.4
  178.0 0.9 fusion.13
  178.9 0.1 multiply_reduce_fusion.3
  179.1 0.9 fusion.14
  180.1 0.1 multiply_reduce_fusion.2
  180.3 0.9 fusion.15
  181.2 0.1 multiply_reduce_fusion.1
  181.4 0.5 multiply_sqrt_fusion
  (31 shorter events, 0.8 us)
Async XLA Ops:
  7.2 98.4 %all-reduce.3.cloned.1.call-start = ((), (), s32[]{:S(2)}) async-start(), calls=%async_computation.1 | async-start | bytes 2097152 | tf_op jit(solution)/shard_map/psum | solution.py:52
  64.1 2.4 %copy-start.2 = (s32[32]{0:T(128)S(1)}, s32[32]{0:T(128)}, u32[]{:S(2)}) copy-start(s32[32]{0:T(128)} %param.5) | copy-start | bytes 388
  64.1 2.4 %copy-start.1 = (s32[32]{0:T(128)S(1)}, s32[32]{0:T(128)}, u32[]{:S(2)}) copy-start(s32[32]{0:T(128)} %param.4) | copy-start | bytes 388
  66.5 100.4 %all-reduce.5.cloned.1.call-start = ((), (), s32[]{:S(2)}) async-start(), calls=%async_computation.2 | async-start | bytes 2097152 | tf_op jit(solution)/shard_map/psum | solution.py:52
  171.1 9.2 %copy-start = (f32[16,64,64]{2,1,0:T(8,128)}, f32[16,64,64]{2,1,0:T(8,128)S(1)}, u32[]{:S(2)}) copy-start(f32[16,64,64]{2,1,0:T(8,128)S(1)} %convolution_multiply_fusion) | copy-start | bytes 786436
Sparse Core Ops, SparseCore 0:
  66.6 38.9 all-reduce.2
  108.1 58.7 all-reduce.4

commit v2 on v0

--- a/solution.py
+++ b/solution.py
@@ -1,3 +1,4 @@
+import functools
 import math
 import jax
 import jax.numpy as jnp
@@ -9,6 +10,14 @@
 POWER = 8
 NF = 128
 power_eps = 1e-06
+
+
+def move_roots(inp, a_name):
+    f_next = jnp.sum(lax.all_gather(inp, a_name), axis=0)
+    return f_next
+
+
+notes_tell = functools.partial(move_roots, a_name=("tm", "pix", "sub"))
 
 
 def window_at(taper_index, steps_t, length):
@@ -46,7 +55,7 @@
     freqs = lax.axis_index("tm") * own + jnp.arange(own, dtype=jnp.int32)
     operator = day_operator(offsets, taper_index, freqs, days, NFFT)
     covariance = jnp.einsum("dp,ep->de", series, series, preferred_element_type=jnp.float32)
-    covariance = lax.psum(covariance, ("tm", "pix", "sub"))
+    covariance = notes_tell(covariance)
     total_pixels = anomaly.shape[1] * lax.axis_size(("pix", "sub"))
     half = jnp.einsum("fid,de->fie", operator, covariance, precision=lax.Precision.HIGH)
     spectral_gram = jnp.einsum("fie,fje->fij", half, operator, precision=lax.Precision.HIGH)

time: 185 us -> 221 us (1.19)
  blocking collectives: 0 us -> 55.2 us
  waiting for transfers between devices: 135 us -> 120 us
  other arithmetic: 8.3 us -> 16.3 us
  starting transfers between devices: 6.49 us -> 0.04 us
  matrix products: 17.3 us -> 13.8 us
    all_gather x0 -> x1, waiting for transfers between devices: none -> 120 us  [move_roots(): f_next = jnp.sum(lax.all_gather(inp, a_name), axis=0)]
    psum x1 -> x0, waiting for transfers between devices: 90.9 us -> none  [shards(): covariance = lax.psum(covariance, ('tm', 'pix', 'sub'))]
    all_to_all x0 -> x1, blocking collectives: none -> 55.2 us  [shards(): lax.all_to_all(anomaly, 'tm', split_axis=1, concat_axis=0, tiled=True)]
    all_to_all x1 -> x0, waiting for transfers between devices: 44.3 us -> none  [shards(): lax.all_to_all(anomaly, 'tm', split_axis=1, concat_axis=0, tiled=True)]
    reduce_sum x0 -> x1, other arithmetic: none -> 7.91 us  [move_roots(): f_next = jnp.sum(lax.all_gather(inp, a_name), axis=0)]
    all_to_all x1 -> x0, starting transfers between devices: 6.46 us -> none  [shards(): lax.all_to_all(anomaly, 'tm', split_axis=1, concat_axis=0, tiled=True)]
    dot_general x1, matrix products: 4.49 us -> 2.27 us  [shards(): jnp.einsum('dp,ep->de', series, series, preferred_element_type=jnp.float32)]
  transfers between devices with their start and end apart: 2 -> 1, of which waited for: 2 -> 1; matrix products, arithmetic and copies ran while one was open for 3% -> 3% of each run, Pallas kernels for 0% -> 0%
where the time goes in v2:
time: 221 us
  waiting for transfers between devices  120 us (54%)
  blocking collectives  55.2 us (25%)
  other arithmetic  16.3 us (7%)
  between operations  14.2 us (6%)
  matrix products  13.8 us (6%)
    all_gather x1, waiting for transfers between devices, move_roots(): f_next = jnp.sum(lax.all_gather(inp, a_name), axis=0)  120 us
    all_to_all x1, blocking collectives, shards(): lax.all_to_all(anomaly, 'tm', split_axis=1, concat_axis=0, tiled=True)  55.2 us
    dot_general x9, matrix products, shards(): jnp.einsum('fij,fj->fi', spectral_gram, vector, precision=lax.Precision.H...  8.61 us
    reduce_sum x1, other arithmetic, move_roots(): f_next = jnp.sum(lax.all_gather(inp, a_name), axis=0)  7.91 us
  transfers between devices with their start and end apart: 1, of which 1 were waited for; matrix products, arithmetic and copies ran while one was open for 3% of the time, Pallas kernels for 0%

profile of v2, /device:TPU:0, one launch (start us, length us, event | category | flops | bytes accessed | tf_op | source)
XLA Modules:
  0.0 221.0 jit_solution(10445171916750966675)
XLA Ops:
  7.2 1.7 copy.28
  8.9 55.2 %all_to_all.19 = bf16[64,8,2048]{2,0,1:T(8,128)(2,1)S(1)} all-to-all(bf16[64,8,2048]{2,0,1:T(8,128)(2,1)S(1)} %bitcast.81), channel_id=1, replica_groups=mesh['group'=2,'tm'=8,'pix'=2,'sub'=1] {'tm'}, dimensions={1} | all-to-all | bytes 4194304 | tf_op jit(solution)/shard_map/all_to_all | solution.py:52
  64.1 2.3 %fusion.6 = f32[512,512]{1,0:T(8,128)} fusion(bf16[512,2048]{1,0:T(8,128)(2,1)S(1)} %bitcast.83), kind=kOutput, calls=%fused_computation.46 | convolution fusion | flops 1073741824 | bytes 3145728 | tf_op jit(solution)/shard_map/dp,ep->de/dot_general | solution.py:57
  66.5 0.9 multiply_reduce_fusion
  67.4 3.8 %fusion.2 = (f32[16,1,32,512]{3,2,1,0:T(8,128)S(1)}, f32[16,1,32,512]{3,2,1,0:T(8,128)S(1)}) fusion(s32[32,512]{1,0:T(8,128)S(1)} %iota_subtract_fusion, s32[16]{0:T(128)S(1)} %iota_add_fusion), kind=kLoop, calls=%fused_computation.8 | loop fusion | flops 1310720 | bytes 2162752 | tf_op jit(solution)/shard_map/cos | solution.py:46
  71.3 0.3 maximum_reduce-precision_fusion
  71.6 0.8 broadcast_multiply_fusion
  72.4 0.3 bitcast_multiply_fusion
  72.7 119.6 %all-gather.3.cloned.1.call-done = f32[8192,512]{1,0:T(8,128)} async-done(((f32[512,512]{1,0:T(8,128)}), f32[8192,512]{1,0:T(8,128)}) %all-gather.3.cloned.1.call-update) | async-done | bytes 16777232 | tf_op jit(solution)/shard_map/all_gather | solution.py:16
  192.3 7.9 %reduce_sum.100 = f32[512,512]{1,0:T(8,128)S(1)} reduce(f32[16,512,512]{2,1,0:T(8,128)} %bitcast.80, f32[]{:T(128)} %constant.54.clone.1), dimensions={0}, to_apply=%region_1.2 | reduce | flops 3932160 | bytes 17825796 | tf_op jit(solution)/shard_map/reduce_sum | solution.py:16
  200.2 1.8 fusion
  202.0 1.1 convolution_multiply_fusion
  203.2 1.1 fusion.7
  204.3 0.1 multiply_reduce_fusion.9
  204.5 0.9 fusion.8
  205.5 0.1 multiply_reduce_fusion.8
  205.7 0.9 fusion.9
  206.6 0.1 multiply_reduce_fusion.7
  206.8 0.9 fusion.10
  207.8 0.1 multiply_reduce_fusion.6
  207.9 0.1 broadcast_divide_fusion.4
  208.0 0.9 fusion.11
  208.9 0.1 multiply_reduce_fusion.5
  209.1 0.9 fusion.12
  210.1 0.1 multiply_reduce_fusion.4
  210.3 0.9 fusion.13
  211.2 0.1 multiply_reduce_fusion.3
  211.4 0.9 fusion.14
  212.4 0.1 multiply_reduce_fusion.2
  212.6 0.9 fusion.15
  213.5 0.1 multiply_reduce_fusion.1
  213.6 0.5 multiply_sqrt_fusion
  (29 shorter events, 0.8 us)
Async XLA Ops:
  7.2 185.1 %all-gather.3.cloned.1.call-start = ((), (), s32[]{:S(2)}) async-start(), calls=%async_computation.1 | async-start | bytes 17825792 | tf_op jit(solution)/shard_map/all_gather | solution.py:16
  64.1 2.3 %copy-start.2 = (s32[32]{0:T(128)S(1)}, s32[32]{0:T(128)}, u32[]{:S(2)}) copy-start(s32[32]{0:T(128)} %param.5) | copy-start | bytes 388
  64.1 2.3 %copy-start.1 = (s32[32]{0:T(128)S(1)}, s32[32]{0:T(128)}, u32[]{:S(2)}) copy-start(s32[32]{0:T(128)} %param.4) | copy-start | bytes 388
  203.2 9.4 %copy-start = (f32[16,64,64]{2,1,0:T(8,128)}, f32[16,64,64]{2,1,0:T(8,128)S(1)}, u32[]{:S(2)}) copy-start(f32[16,64,64]{2,1,0:T(8,128)S(1)} %convolution_multiply_fusion) | copy-start | bytes 786436
Sparse Core Ops, SparseCore 0:
  66.6 125.6 all-gather.2
